TPU v7x, 128 devices: a whole 4x4x4 slice. The times are simulated.
128 devices in a mesh: row: 8 (over z, core), col: 16 (over x, y).
Axes of the slice: x: 4, y: 4, z: 4, core: 2. Of those that a mesh axis runs over, the one named last changes fastest.
Arguments:
- obj_re: float32 [4096, 8192], P('row', 'col'), may hold values from -4 to 4
- obj_im: float32 [4096, 8192], P('row', 'col'), may hold values from -4 to 4
- probe_re: float32 [512, 512], replicated, may hold values from -6 to 6
- probe_im: float32 [512, 512], replicated, may hold values from -6 to 6
- amplitude: bfloat16 [8, 64, 512, 512], P('row', 'col'), may hold values from 0.099609375 to 3
- offset_y: int32 [8, 64], P('row', 'col'), may hold values from 0 to 511
- offset_x: int32 [8, 64], P('row', 'col'), may hold values from 0 to 511
- counts: int32 [8, 16], P('row', 'col'), may hold values from 1 to 4, as said below
Outputs:
- new_re: float32 [4096, 8192], P('row', 'col')
- new_im: float32 [4096, 8192], P('row', 'col')
Inputs may be any that keep to these rules, and one draw needn't show every extreme that they name: The live slots of a device are its first counts[r, c] slots; some device has 4 live slots. `offset_y`: A window starts inside the tile of the device that holds its slot.
All inputs are finite; a program needn't handle non-finite values.
Results may differ from a plain program's by a relative error of at most 0.0024.
The roundings to bfloat16 on the way count: a program that leaves them out, or rounds other values in their place, can miss the bound.
Values may be sent and summed in bfloat16 or wider, within the bound.
A program may use at most 128 MiB of HBM per device.

v0:
```python
import math

import jax
import jax.numpy as jnp
from jax import lax
from jax.sharding import PartitionSpec as P

modulus_floor = 0.5
shrink_level = 0.2
step_size = 0.5
epsilon = 1e-05


def passed_along(value, axis, steps):
    count = lax.axis_size(axis)
    pairs = [(source, (source + steps) % count) for source in range(count)]
    return lax.ppermute(value, axis, pairs)


def with_halo(cells, sides, width):
    for axis, dim in sides:
        count = lax.axis_size(axis)
        head = lax.slice_in_dim(cells, 0, width, axis=dim)
        tail = lax.slice_in_dim(cells, cells.shape[dim] - width, cells.shape[dim], axis=dim)
        cells = jnp.concatenate(
            [
                lax.ppermute(tail, axis, [(i, (i + 1) % count) for i in range(count)]),
                cells,
                lax.ppermute(head, axis, [((i + 1) % count, i) for i in range(count)]),
            ],
            axis=dim,
        )
    return cells


def dft_tables(pattern_side):
    ordinal = jnp.arange(pattern_side, dtype=jnp.int32)
    phase_index = ordinal[:, None] * ordinal[None, :] % pattern_side
    angles = phase_index.astype(jnp.float32) * (2.0 * math.pi / pattern_side)
    norming = 1.0 / math.sqrt(pattern_side)
    return (
        (jnp.cos(angles) * norming).astype(jnp.bfloat16),
        (-jnp.sin(angles) * norming).astype(jnp.bfloat16),
    )


def matmul(left_op, right_op):
    return jnp.dot(left_op, right_op, preferred_element_type=jnp.float32)


def spectrum_rows(patch_tile, probe_re, probe_im, cos_table, sin_table):
    object_re = patch_tile[0].astype(jnp.float32)
    object_im = patch_tile[1].astype(jnp.float32)
    exit_re = (probe_re * object_re - probe_im * object_im).astype(jnp.bfloat16)
    exit_im = (probe_re * object_im + probe_im * object_re).astype(jnp.bfloat16)
    half_re = matmul(cos_table, exit_re) - matmul(sin_table, exit_im)
    half_im = matmul(cos_table, exit_im) + matmul(sin_table, exit_re)
    return jnp.stack([half_re, half_im]).astype(jnp.bfloat16)


def correct_rows(half_spec, measured, cos_table, sin_table):
    spec_re = matmul(half_spec[0], cos_table) - matmul(half_spec[1], sin_table)
    spec_im = matmul(half_spec[0], sin_table) + matmul(half_spec[1], cos_table)
    modulus = jnp.sqrt(spec_re * spec_re + spec_im * spec_im)
    factor = measured.astype(jnp.float32) / jnp.maximum(modulus, modulus_floor) - 1.0
    delta_re = (spec_re * factor).astype(jnp.bfloat16)
    delta_im = (spec_im * factor).astype(jnp.bfloat16)
    back_re = matmul(delta_re, cos_table) + matmul(delta_im, sin_table)
    back_im = matmul(delta_im, cos_table) - matmul(delta_re, sin_table)
    return jnp.stack([back_re, back_im]).astype(jnp.bfloat16)


def object_term(partial_back, probe_re, probe_im, cos_table, sin_table):
    wave_re = matmul(cos_table, partial_back[0]) + matmul(sin_table, partial_back[1])
    wave_im = matmul(cos_table, partial_back[1]) - matmul(sin_table, partial_back[0])
    return jnp.stack(
        [probe_re * wave_re + probe_im * wave_im, probe_re * wave_im - probe_im * wave_re]
    )


def shrink(entries):
    return entries - jnp.clip(entries, -shrink_level, shrink_level)


def haar_clean(field):
    top_left = field[:, 0::2, 0::2]
    top_right = field[:, 0::2, 1::2]
    low_left = field[:, 1::2, 0::2]
    low_right = field[:, 1::2, 1::2]
    coarse = 0.5 * (top_left + top_right + low_left + low_right)
    across = shrink(0.5 * (top_left - top_right + low_left - low_right))
    downward = shrink(0.5 * (top_left + top_right - low_left - low_right))
    diagonal = shrink(0.5 * (top_left - top_right - low_left + low_right))
    new_top_left = 0.5 * (coarse + across + downward + diagonal)
    new_top_right = 0.5 * (coarse - across + downward - diagonal)
    new_low_left = 0.5 * (coarse + across - downward - diagonal)
    new_low_right = 0.5 * (coarse - across - downward + diagonal)
    planes, height, breadth = top_left.shape
    top_rows = jnp.stack([new_top_left, new_top_right], axis=-1).reshape(
        planes, height, 2 * breadth
    )
    bottom_rows = jnp.stack([new_low_left, new_low_right], axis=-1).reshape(
        planes, height, 2 * breadth
    )
    return jnp.stack([top_rows, bottom_rows], axis=2).reshape(planes, 2 * height, 2 * breadth)


def body(obj_re, obj_im, probe_re, probe_im, amplitude, offset_y, offset_x, counts):
    pattern_side = probe_re.shape[0]
    cos_table, sin_table = dft_tables(pattern_side)
    probe_power = jnp.mean(probe_re * probe_re + probe_im * probe_im) + epsilon
    anchor = jnp.int32(0)
    own_tile = jnp.stack([obj_re, obj_im]).astype(jnp.bfloat16)
    right_tile = passed_along(own_tile, "col", -1)
    tile_strip = jnp.concatenate([own_tile, right_tile], axis=2)
    below_pair = passed_along(tile_strip, "row", -1)
    region = jnp.concatenate([tile_strip, below_pair], axis=1)
    live_count = counts[0, 0]

    def whole_slot(slot_index, accumulated):
        row_at = offset_y[0, slot_index]
        col_at = offset_x[0, slot_index]
        patch_tile = lax.dynamic_slice(
            region, (anchor, row_at, col_at), (2, pattern_side, pattern_side)
        )
        half_spec = spectrum_rows(patch_tile, probe_re, probe_im, cos_table, sin_table)
        partial_back = correct_rows(half_spec, amplitude[0, slot_index], cos_table, sin_table)
        update = object_term(partial_back, probe_re, probe_im, cos_table, sin_table)
        window = lax.dynamic_slice(
            accumulated, (anchor, row_at, col_at), (2, pattern_side, pattern_side)
        )
        return lax.dynamic_update_slice(accumulated, window + update, (anchor, row_at, col_at))

    empty_sums = jnp.zeros((2, 2 * pattern_side, 2 * pattern_side), jnp.float32)
    accumulated = lax.fori_loop(0, live_count, whole_slot, empty_sums)
    lower_part = passed_along(accumulated[:, pattern_side:, :], "row", 1)
    upper_part = accumulated[:, :pattern_side, :] + lower_part
    spill_over = passed_along(upper_part[:, :, pattern_side:], "col", 1)
    intersection = upper_part[:, :, :pattern_side] + spill_over
    half_step = jnp.stack([obj_re, obj_im]) + step_size / probe_power * intersection
    rimmed = with_halo(half_step, (("row", 1), ("col", 2)), 1)
    cleaned = 0.5 * (
        haar_clean(half_step) + haar_clean(rimmed)[:, 1 : pattern_side + 1, 1 : pattern_side + 1]
    )
    return (cleaned[0], cleaned[1])


def solution(mesh):
    return jax.shard_map(
        body,
        mesh=mesh,
        in_specs=(
            P("row", "col"),
            P("row", "col"),
            P(),
            P(),
            P("row", "col", None, None),
            P("row", "col"),
            P("row", "col"),
            P("row", "col"),
        ),
        out_specs=(P("row", "col"), P("row", "col")),
        check_vma=False,
    )
```

profile of v0, /device:TPU:0, one launch (start us, length us, event | category | flops | bytes accessed | tf_op | source)
XLA Modules:
  0.0 859.8 jit_solution(2406121443305844054)
XLA Ops:
  3.3 5.3 collective-permute-start
  8.6 22.4 %collective-permute-done = bf16[2,512,512]{1,2,0:T(8,128)(2,1)S(1)} collective-permute-done((bf16[2,512,512]{1,2,0:T(8,128)(2,1)S(1)}, bf16[2,512,512]{1,2,0:T(8,128)(2,1)S(1)}, u32[]{:S(2)}, u32[]{:S(2)}) %collective-permute-start) | collective-permute-done | bytes 1048608 | tf_op jit(solution)/shard_map/ppermute | solution.py:17
  39.5 19.7 %collective-permute-done.1 = bf16[2,512,1024]{1,2,0:T(8,128)(2,1)} collective-permute-done((bf16[2,512,1024]{1,2,0:T(8,128)(2,1)}, bf16[2,512,1024]{1,2,0:T(8,128)(2,1)}, u32[]{:S(2)}, u32[]{:S(2)}) %collective-permute-start.1) | collective-permute-done | bytes 2097184 | tf_op jit(solution)/shard_map/ppermute | solution.py:17
  67.0 244.5 %while.14 = (s32[]{:T(128)}, f32[2,1024,1024]{1,2,0:T(8,128)}, s32[]{:T(128)}, s32[1,4]{1,0:T(1,128)S(1)}, s32[1,4]{1,0:T(1,128)S(1)}, /*index=5*/bf16[2,1024,10...) while((s32[]{:T(128)}, f32[2,1024,1024]{1,2,0:T(8,128)}, ...), condition=%wide.region_2.3_spmd.clone.clone, body=%wide.region_1.2_spmd.clone.clone.sunk | while | flops 4375445504 | bytes 51904804 | solution.py:135
  115.8 5.0 fusion.180
  120.8 5.2 convolution_subtract_fusion.5
  126.0 5.1 fusion.183
  131.1 6.2 multiply_convert_fusion.53
  152.1 5.0 fusion.185
  162.1 5.2 fusion.189
  172.3 6.0 add_bitcast_fusion.2
  180.8 14.4 %dynamic_update_slice.9 = f32[2,1024,1024]{1,2,0:T(8,128)} dynamic-update-slice(f32[2,1024,1024]{1,2,0:T(8,128)} %get-tuple-element.415, f32[2,512,512]{1,2,0:T(8,128)S(1)} %maximum_add_fusion.2, s32[]{:T(128)} %constant.61.clone.1..sunk, s32[]{:T(128)S(6)} %select_n.141, s32[]{:T(128)S(6)} %select_n.142) | dynamic-update-slice | bytes 4194308 | tf_op jit(solution)/shard_map/while/body/dynamic_update_slice | solution.py:132
  222.3 5.0 fusion.180
  227.4 5.2 convolution_subtract_fusion.5
  232.6 5.1 fusion.183
  237.6 6.2 multiply_convert_fusion.53
  268.7 5.2 fusion.189
  278.9 6.0 add_bitcast_fusion.2
  287.4 14.1 %dynamic_update_slice.9 = f32[2,1024,1024]{1,2,0:T(8,128)} dynamic-update-slice(f32[2,1024,1024]{1,2,0:T(8,128)} %get-tuple-element.415, f32[2,512,512]{1,2,0:T(8,128)S(1)} %maximum_add_fusion.2, s32[]{:T(128)} %constant.61.clone.1..sunk, s32[]{:T(128)S(6)} %select_n.141, s32[]{:T(128)S(6)} %select_n.142) | dynamic-update-slice | bytes 4194308 | tf_op jit(solution)/shard_map/while/body/dynamic_update_slice | solution.py:132
  314.3 49.1 %collective-permute-done.2 = f32[2,512,1024]{1,2,0:T(8,128)S(1)} collective-permute-done((f32[2,512,1024]{1,2,0:T(8,128)S(1)}, f32[2,512,1024]{1,2,0:T(8,128)S(1)}, u32[]{:S(2)}, u32[]{:S(2)}) %collective-permute-start.2) | collective-permute-done | bytes 4194336 | tf_op jit(solution)/shard_map/ppermute | solution.py:17
  366.6 210.3 %collective-permute-start.3 = (f32[2,512,512]{1,2,0:T(8,128)S(1)}, f32[2,512,512]{1,2,0:T(8,128)}, u32[]{:S(2)}, u32[]{:S(2)}) collective-permute-start(f32[2,512,512]{1,2,0:T(8,128)S(1)} %slice.113), channel_id=1, source_target_pairs={{0,1},{1,2},{2,3},{3,4},{4,5},{5,6},{6,7},{7,8},{8,9},{9,10},{10,1... | collective-permute-start | bytes 6291464 | tf_op jit(solution)/shard_map/ppermute | solution.py:17
  578.5 40.6 %collective-permute-done.3 = f32[2,512,512]{1,2,0:T(8,128)} collective-permute-done((f32[2,512,512]{1,2,0:T(8,128)S(1)}, f32[2,512,512]{1,2,0:T(8,128)}, u32[]{:S(2)}, u32[]{:S(2)}) %collective-permute-start.3) | collective-permute-done | bytes 2097184 | tf_op jit(solution)/shard_map/ppermute | solution.py:17
  622.4 23.6 %slice.93 = f32[2,256,256]{1,2,0:T(8,128)S(1)} slice(f32[2,512,512]{1,2,0:T(8,128)S(1)} %fusion.111), slice={[0:2:1], [0:512:2], [0:512:2]} | slice | bytes 1048576 | tf_op jit(solution)/shard_map/slice | solution.py:86
  646.0 23.6 %slice.94 = f32[2,256,256]{1,2,0:T(8,128)S(1)} slice(f32[2,512,512]{1,2,0:T(8,128)S(1)} %fusion.111), slice={[0:2:1], [0:512:2], [1:512:2]} | slice | bytes 1048576 | tf_op jit(solution)/shard_map/slice | solution.py:87
  669.6 24.1 %slice.95 = f32[2,256,256]{1,2,0:T(8,128)} slice(f32[2,512,512]{1,2,0:T(8,128)S(1)} %fusion.111), slice={[0:2:1], [1:512:2], [0:512:2]} | slice | bytes 1048576 | tf_op jit(solution)/shard_map/slice | solution.py:88
  693.7 24.3 %slice.96 = f32[2,256,256]{1,2,0:T(8,128)} slice(f32[2,512,512]{1,2,0:T(8,128)S(1)} %fusion.111), slice={[0:2:1], [1:512:2], [1:512:2]} | slice | bytes 1048576 | tf_op jit(solution)/shard_map/slice | solution.py:89
  737.3 6.5 copy.29
  746.2 23.4 %slice.101 = f32[2,257,257]{1,2,0:T(8,128)S(1)} slice(f32[2,514,514]{1,2,0:T(8,128)} %pad_maximum_fusion.2), slice={[0:2:1], [0:514:2], [0:514:2]} | slice | bytes 1056784 | tf_op jit(solution)/shard_map/slice | solution.py:86
  769.6 23.7 %slice.102 = f32[2,257,257]{1,2,0:T(8,128)} slice(f32[2,514,514]{1,2,0:T(8,128)} %pad_maximum_fusion.2), slice={[0:2:1], [0:514:2], [1:514:2]} | slice | bytes 1056784 | tf_op jit(solution)/shard_map/slice | solution.py:87
  793.4 23.3 %slice.103 = f32[2,257,257]{1,2,0:T(8,128)} slice(f32[2,514,514]{1,2,0:T(8,128)S(1)} %copy-done.2), slice={[0:2:1], [1:514:2], [0:514:2]} | slice | bytes 1056784 | tf_op jit(solution)/shard_map/slice | solution.py:88
  816.7 23.4 %slice.104 = f32[2,257,257]{1,2,0:T(8,128)} slice(f32[2,514,514]{1,2,0:T(8,128)S(1)} %copy-done.2), slice={[0:2:1], [1:514:2], [1:514:2]} | slice | bytes 1056784 | tf_op jit(solution)/shard_map/slice | solution.py:89
  846.0 5.2 copy.32
  (105 shorter events, 169.9 us)
Async XLA Ops:
  0.6 1.7 copy-start.16
  2.3 1.0 copy-start.3
  2.6 30.0 %copy-start.5 = (f32[512,512]{0,1:T(8,128)}, f32[512,512]{0,1:T(8,128)S(1)}, u32[]{:S(2)}) copy-start(f32[512,512]{0,1:T(8,128)S(1)} %copy.24) | copy-start | bytes 3145732
  3.3 27.7 %collective-permute-start = (bf16[2,512,512]{1,2,0:T(8,128)(2,1)S(1)}, bf16[2,512,512]{1,2,0:T(8,128)(2,1)S(1)}, u32[]{:S(2)}, u32[]{:S(2)}) collective-permute-start(bf16[2,512,512]{1,2,0:T(8,128)(2,1)S(1)} %fusion.112), channel_id=1, source_target_pairs={{0,15},{1,0},{2,1},{3,2},{4,3},{5,4},{6,5},{7,6},{8,7},{9,8},{10,9... | collective-permute-start | bytes 3145736 | tf_op jit(solution)/shard_map/ppermute | solution.py:17
  31.0 1.7 copy-start.8
  32.7 26.5 %collective-permute-start.1 = (bf16[2,512,1024]{1,2,0:T(8,128)(2,1)}, bf16[2,512,1024]{1,2,0:T(8,128)(2,1)}, u32[]{:S(2)}, u32[]{:S(2)}) collective-permute-start(bf16[2,512,1024]{1,2,0:T(8,128)(2,1)} %pad_maximum_fusion.4), channel_id=1, source_target_pairs={{0,112},{16,0},{32,16},{48,32},{64,48},{80,64},{96,80},{112,96},{1... | collective-permute-start | bytes 6291464 | tf_op jit(solution)/shard_map/ppermute | solution.py:17
  35.3 23.9 %copy-start.9 = (bf16[2,512,512]{1,2,0:T(8,128)(2,1)S(1)}, bf16[2,512,512]{1,2,0:T(8,128)(2,1)}, u32[]{:S(2)}) copy-start(bf16[2,512,512]{1,2,0:T(8,128)(2,1)} %copy-done.8) | copy-start | bytes 3145732
  62.6 4.3 copy-start.17
  62.6 4.3 copy-start.18
  311.5 52.0 %copy-start = (f32[2,1024,1024]{1,2,0:T(8,128)S(1)}, f32[2,1024,1024]{1,2,0:T(8,128)}, u32[]{:S(2)}) copy-start(f32[2,1024,1024]{1,2,0:T(8,128)} %get-tuple-element.184) | copy-start | bytes 25165828
  314.3 49.2 %collective-permute-start.2 = (f32[2,512,1024]{1,2,0:T(8,128)S(1)}, f32[2,512,1024]{1,2,0:T(8,128)S(1)}, u32[]{:S(2)}, u32[]{:S(2)}) collective-permute-start(f32[2,512,1024]{1,2,0:T(8,128)S(1)} %slice.90), channel_id=1, source_target_pairs={{0,16},{16,32},{32,48},{48,64},{64,80},{80,96},{96,112},{112,0},{1... | collective-permute-start | bytes 12582920 | tf_op jit(solution)/shard_map/ppermute | solution.py:17
  364.5 2.1 copy-start.1
  364.5 212.4 %copy-start.6 = (f32[512,512]{1,0:T(8,128)S(1)}, f32[512,512]{1,0:T(8,128)}, u32[]{:S(2)}) copy-start(f32[512,512]{1,0:T(8,128)} %param.12) | copy-start | bytes 3145732
  364.5 212.4 %copy-start.7 = (f32[512,512]{1,0:T(8,128)S(1)}, f32[512,512]{1,0:T(8,128)}, u32[]{:S(2)}) copy-start(f32[512,512]{1,0:T(8,128)} %param.13) | copy-start | bytes 3145732
  366.6 252.5 %copy-start.4 = (f32[512,512]{0,1:T(8,128)S(1)}, f32[512,512]{0,1:T(8,128)}, u32[]{:S(2)}) copy-start(f32[512,512]{0,1:T(8,128)} %copy-done.3) | copy-start | bytes 3145732
  366.6 252.5 %collective-permute-start.3 = (f32[2,512,512]{1,2,0:T(8,128)S(1)}, f32[2,512,512]{1,2,0:T(8,128)}, u32[]{:S(2)}, u32[]{:S(2)}) collective-permute-start(f32[2,512,512]{1,2,0:T(8,128)S(1)} %slice.113), channel_id=1, source_target_pairs={{0,1},{1,2},{2,3},{3,4},{4,5},{5,6},{6,7},{7,8},{8,9},{9,10},{10,1... | collective-permute-start | bytes 6291464 | tf_op jit(solution)/shard_map/ppermute | solution.py:17
  717.9 3.2 copy-start.10
  717.9 3.2 copy-start.11
  718.1 9.8 %collective-permute-start.4 = (f32[2,1,512]{1,2,0:T(8,128)S(1)}, f32[2,1,512]{1,2,0:T(8,128)S(1)}, u32[]{:S(2)}, u32[]{:S(2)}) collective-permute-start(f32[2,1,512]{1,2,0:T(8,128)S(1)} %get-tuple-element.322), channel_id=1, source_target_pairs={{0,16},{16,32},{32,48},{48,64},{64,80},{80,96},{96,112},{112,0},{1... | collective-permute-start | bytes 12296 | tf_op jit(solution)/shard_map/ppermute | solution.py:27
  718.2 9.8 %collective-permute-start.5 = (f32[2,1,512]{1,2,0:T(8,128)S(1)}, f32[2,1,512]{1,2,0:T(8,128)S(1)}, u32[]{:S(2)}, u32[]{:S(2)}) collective-permute-start(f32[2,1,512]{1,2,0:T(8,128)S(1)} %get-tuple-element.323), channel_id=1, source_target_pairs={{16,0},{32,16},{48,32},{64,48},{80,64},{96,80},{112,96},{0,112},{1... | collective-permute-start | bytes 12296 | tf_op jit(solution)/shard_map/ppermute | solution.py:29
  728.0 0.8 copy-start.12
  728.8 0.8 copy-start.14
  729.6 14.2 %collective-permute-start.6 = (f32[2,514,1]{1,2,0:T(1,128)S(1)}, f32[2,514,1]{1,2,0:T(1,128)S(1)}, u32[]{:S(2)}, u32[]{:S(2)}) collective-permute-start(f32[2,514,1]{1,2,0:T(1,128)S(1)} %get-tuple-element.315), channel_id=1, source_target_pairs={{0,1},{1,2},{2,3},{3,4},{4,5},{5,6},{6,7},{7,8},{8,9},{9,10},{10,1... | collective-permute-start | bytes 12344 | tf_op jit(solution)/shard_map/ppermute | solution.py:27
  732.1 11.6 %collective-permute-start.7 = (f32[2,514,1]{1,2,0:T(1,128)S(1)}, f32[2,514,1]{1,2,0:T(1,128)S(1)}, u32[]{:S(2)}, u32[]{:S(2)}) collective-permute-start(f32[2,514,1]{1,2,0:T(1,128)S(1)} %get-tuple-element.316), channel_id=1, source_target_pairs={{1,0},{2,1},{3,2},{4,3},{5,4},{6,5},{7,6},{8,7},{9,8},{10,9},{11,1... | collective-permute-start | bytes 12344 | tf_op jit(solution)/shard_map/ppermute | solution.py:29
  737.3 6.5 copy-start.13
  737.3 6.5 copy-start.15
  746.2 47.1 %copy-start.2 = (f32[2,514,514]{1,2,0:T(8,128)S(1)}, f32[2,514,514]{1,2,0:T(8,128)}, u32[]{:S(2)}) copy-start(f32[2,514,514]{1,2,0:T(8,128)} %pad_maximum_fusion.2) | copy-start | bytes 6340708
where the time goes:
time: 868 us; the launch traced here: 860 us
  local copies, waits for them, and re-layouts  255 us (29%)
  starting transfers between devices  227 us (26%)
  matrix products  165 us (19%)
  waiting for transfers between devices  136 us (16%)
  loops' own time  40.5 us (5%)
  other arithmetic  34.7 us (4%)
    ppermute x4, starting transfers between devices, passed_along(): return lax.ppermute(value, axis, pairs)  218 us
    dot_general x32, matrix products, matmul(): return jnp.dot(left_op, right_op, preferred_element_type=jnp.float32)  165 us
    ppermute x4, waiting for transfers between devices, passed_along(): return lax.ppermute(value, axis, pairs)  132 us
    slice x2, local copies, waits for them, and re-layouts, haar_clean(): low_right = field[:, 1::2, 1::2]  47.7 us
    slice x2, local copies, waits for them, and re-layouts, haar_clean(): low_left = field[:, 1::2, 0::2]  47.4 us
    slice x2, local copies, waits for them, and re-layouts, haar_clean(): top_right = field[:, 0::2, 1::2]  47.3 us
    slice x2, local copies, waits for them, and re-layouts, haar_clean(): top_left = field[:, 0::2, 0::2]  47 us
    another operation x1, loops' own time, body(): accumulated = lax.fori_loop(0, live_count, whole_slot, empty_sums)  40.5 us
  transfers between devices with their start and end apart: 8, of which 5 were waited for; matrix products, arithmetic and copies ran while one was open for 2% of the time, Pallas kernels for 0%

commit v1 on v0

v1 whole, which is shorter than its diff:
```python
import math

import jax
import jax.numpy as jnp
import ml_dtypes
import numpy as np
from jax import lax
from jax.experimental import pallas as pl
from jax.experimental.pallas import tpu as pltpu
from jax.sharding import PartitionSpec as P

SIDE = 512
QUARTER = 128
HALF = 256
SLOTS = 4
EPS = 1e-05
STEP = 0.5
SHRINK = 0.2
BF = jnp.bfloat16
F32 = jnp.float32
MESH = pl.DeviceIdType.MESH


def tables():
    phase = np.arange(SIDE) * (2.0 * math.pi / SIDE)
    norming = 1.0 / math.sqrt(SIDE)
    cosine = (np.cos(phase) * norming).astype(np.float32)
    sine = (-np.sin(phase) * norming).astype(np.float32)
    quarter = np.arange(4) * QUARTER
    cosine[quarter[1::2]] = 0.0
    sine[quarter[0::2]] = 0.0

    def entries(rows, cols):
        at = np.outer(rows, cols) % SIDE
        return cosine[at], sine[at]

    natural = np.arange(SIDE)
    by_class = np.concatenate([natural[m::4] for m in range(4)])
    block = np.concatenate([np.arange(m, QUARTER, 4) for m in range(4)])
    even, odd = np.arange(0, HALF, 2), np.arange(1, HALF, 2)
    minus_even = (SIDE - even) % SIDE
    minus_even[0] = HALF
    freq = np.concatenate([even, odd, minus_even, SIDE - odd])
    c, s = entries(block, by_class)
    first = np.concatenate([c, s], axis=0)
    c, s = entries(natural, freq[:HALF])
    s[:, 0] = entries(natural, np.array([HALF]))[0][:, 0]
    second = np.concatenate([c, s], axis=1)
    c, s = entries(freq, natural)
    third = np.concatenate([c, s], axis=0)
    c, s = entries(natural, by_class)
    fourth = np.concatenate([c, s], axis=1)
    return [t.astype(ml_dtypes.bfloat16) for t in (first, second, third, fourth)]


def dot(a, b):
    return jnp.dot(a, b, preferred_element_type=F32)


def iota(shape, dim):
    return lax.broadcasted_iota(jnp.int32, shape, dim)


def strided(ref, p, start, size):
    return jnp.concatenate([ref[p, k, pl.ds(start, size, stride=4), :] for k in range(4)], axis=1)


def one_hot(hit):
    return jnp.where(hit, 1.0, 0.0).astype(BF)


def kernel(offy, offx, cnt, objr, obji, prbr, prbi, amp, b1h, b2h, b3h, b4h,
           outr, outi,
           objn, tile, prbn, prot, ampr, ampp, b1, b2, b3, b4,
           t1, t2, t3, t4, gbuf, half, back, dbuf, term,
           slr, sur, sll, rlr, rll, rur, hs, ext, res, outn,
           msg, halo, colt, power,
           insem, outsem, fs, fr, bs, br, hsem, hrem):
    nr, nc = lax.axis_size("row"), lax.axis_size("col")
    r, c = lax.axis_index("row"), lax.axis_index("col")
    up, down = lax.rem(r + nr - 1, nr), lax.rem(r + 1, nr)
    left, right = lax.rem(c + nc - 1, nc), lax.rem(c + 1, nc)

    moves = []
    for ref, dst, p in ((objr, objn, 0), (obji, objn, 1), (prbr, prbn, 0), (prbi, prbn, 1)):
        moves += [(ref.at[:, k * QUARTER:(k + 1) * QUARTER], dst.at[p, k]) for k in range(4)]
    moves += [(amp.at[0], ampr), (b1h, b1), (b2h, b2), (b3h, b3), (b4h, b4)]
    ins = [pltpu.make_async_copy(a, b, insem.at[i]) for i, (a, b) in enumerate(moves)]
    for copy in ins:
        copy.start()

    barrier = pltpu.get_barrier_semaphore()
    for rr in (up, r, down):
        for cc in (left, c, right):
            if rr is r and cc is c:
                continue
            pl.semaphore_signal(barrier, inc=1, device_id=(rr, cc), device_id_type=MESH)

    def remote(src, dst, ssem, rsem, rr, cc):
        return pltpu.make_async_remote_copy(src_ref=src, dst_ref=dst, send_sem=ssem, recv_sem=rsem,
                                            device_id=(rr, cc), device_id_type=MESH)

    def to_left(p, m):
        return remote(tile.at[0, p, m], tile.at[1, p, m], fs.at[0, p, m], fr.at[0, p, m], r, left)

    def to_up(p, m):
        return remote(tile.at[0, p, m], tile.at[2, p, m], fs.at[1, p, m], fr.at[1, p, m], up, c)

    def pass_up(p, m):
        return remote(tile.at[1, p, m], tile.at[3, p, m], fs.at[2, p, m], fr.at[2, p, m], up, c)

    chunks = [(p, m) for p in range(2) for m in range(4)]
    for p in range(2):
        for copy in ins[4 * p:4 * p + 4]:
            copy.wait()
        for m in range(4):
            tile[0, p, m] = strided(objn, p, m, QUARTER).astype(BF)
            if p == 0 and m == 0:
                pl.semaphore_wait(barrier, 8)
            to_left(p, m).start()
            to_up(p, m).start()
    for copy in ins[8:]:
        copy.wait()

    total = jnp.zeros((8, SIDE), F32)
    for p in range(2):
        def add(i, acc, p=p):
            x = jnp.concatenate([prbn[p, k, pl.ds(pl.multiple_of(i * 8, 8), 8), :] for k in range(4)], axis=1)
            return acc + x * x
        total = lax.fori_loop(0, SIDE // 8, add, total)
    mean = jnp.sum(jnp.sum(total, axis=1, keepdims=True), axis=0, keepdims=True) * (1.0 / (SIDE * SIDE)) + EPS
    power[...] = jnp.broadcast_to(STEP / mean, (8, QUARTER))

    def prepare(s):
        oy, ox = offy[0, s], offx[0, s]
        live = jnp.where(s < cnt[0, 0], 1.0, 0.0).astype(F32)
        lam, freq = iota((SIDE, SIDE), 1), iota((SIDE, SIDE), 0)
        lane = lam & 127
        even_minus = jnp.where(lane == 0, HALF, SIDE - 2 * lane)
        want = jnp.where(lam < 128, 2 * lane,
                         jnp.where(lam < 256, 2 * lane + 1,
                                   jnp.where(lam < 384, even_minus, SIDE - 1 - 2 * lane)))
        mixed = dot(ampr[s], one_hot(freq == want)).astype(BF)
        pick = one_hot(lam == 4 * (freq & 127) + (freq >> 7))
        ampp[s] = dot(pick, mixed).astype(BF).reshape(4, QUARTER, SIDE)
        for m in range(4):
            turn = lax.shift_right_logical(oy + m, 2) & 127
            for p in range(2):
                x = strided(prbn, p, m, QUARTER) * live
                prot[s, p, m] = pltpu.roll(pltpu.roll(x, turn, 0), ox, 1)
            cs = pltpu.roll(b1[:, m * QUARTER:(m + 1) * QUARTER].astype(F32), turn, 1)
            cc, ss = cs[:QUARTER], cs[QUARTER:]
            t1[s, m] = jnp.concatenate([jnp.concatenate([cc, -ss], axis=1),
                                        jnp.concatenate([ss, cc], axis=1)], axis=0).astype(BF)
        rows, cols = iota((SIDE, SIDE), 0), iota((SIDE, SIDE), 1)
        t2[s] = dot(one_hot(cols == ((rows - ox) & 511)), b2[...]).astype(BF)
        rows, cols = iota((SIDE, HALF), 0), iota((SIDE, HALF), 1)
        cs = dot(b3[...], one_hot(rows == ((cols - ox) & 511)))
        for par in range(2):
            a = par * QUARTER
            cc = jnp.concatenate([cs[a:a + 128], cs[a + 256:a + 384]], axis=0)
            ss = jnp.concatenate([cs[a + 512:a + 640], cs[a + 768:a + 896]], axis=0)
            t3[s, par] = jnp.concatenate([jnp.concatenate([cc, -ss], axis=1),
                                          jnp.concatenate([ss, cc], axis=1)], axis=0).astype(BF)
        rows, cols = iota((QUARTER, SIDE), 0), iota((QUARTER, SIDE), 1)
        place = 4 * (rows & 31) + lax.shift_right_logical(rows, 5)
        cs = dot(one_hot(cols == ((place - oy) & 511)), b4[...])
        for m in range(4):
            cc = cs[:, m * QUARTER:(m + 1) * QUARTER]
            ss = cs[:, SIDE + m * QUARTER:SIDE + (m + 1) * QUARTER]
            t4[s, m] = jnp.concatenate([jnp.concatenate([cc, ss], axis=1),
                                        jnp.concatenate([-ss, cc], axis=1)], axis=0).astype(BF)

    def prepare_and_pass(s, carry):
        prepare(s)
        p, m = s // 2, 2 * (s % 2)
        for k in range(2):
            to_left(p, m + k).wait_recv()
            pass_up(p, m + k).start()
        return carry

    lax.fori_loop(0, SLOTS, prepare_and_pass, 0)
    for p, m in chunks:
        to_up(p, m).wait_recv()
    for p, m in chunks:
        pass_up(p, m).wait_recv()

    def one_slot(s, carry):
        oy, ox = offy[0, s], offx[0, s]
        for h in range(2):
            cols = slice(h * HALF, (h + 1) * HALF)
            for m in range(4):
                mu = (m + oy) & 3
                xs = []
                for i in range(0, QUARTER, 32):
                    rs = slice(i, i + 32)
                    own_row = 4 * (iota((32, HALF), 0) + i) + mu >= oy
                    own_col = iota((32, HALF), 1) + h * HALF >= ox
                    part = []
                    for p in range(2):
                        q = [tile[k, p, mu, rs, cols].astype(F32) for k in range(4)]
                        part.append(jnp.where(own_row, jnp.where(own_col, q[0], q[1]),
                                              jnp.where(own_col, q[2], q[3])))
                    pr, pi = prot[s, 0, m, rs, cols], prot[s, 1, m, rs, cols]
                    xs.append(((pr * part[0] - pi * part[1]).astype(BF), (pr * part[1] + pi * part[0]).astype(BF)))
                x = jnp.concatenate([a for a, _ in xs] + [b for _, b in xs], axis=0)
                gbuf[m] = dot(t1[s, m], x)
            for i in range(0, QUARTER, 32):
                re, im = slice(i, i + 32), slice(QUARTER + i, QUARTER + i + 32)
                g = [(gbuf[m, re, :], gbuf[m, im, :]) for m in range(4)]
                ar, ai = g[0][0] + g[2][0], g[0][1] + g[2][1]
                br_, bi_ = g[0][0] - g[2][0], g[0][1] - g[2][1]
                cr, ci = g[1][0] + g[3][0], g[1][1] + g[3][1]
                dr, di = g[1][0] - g[3][0], g[1][1] - g[3][1]
                mm = i // 32
                for q, (xr, xi) in enumerate([(ar + cr, ai + ci), (br_ + di, bi_ - dr),
                                              (ar - cr, ai - ci), (br_ - di, bi_ + dr)]):
                    half[0, mm, q * 32:(q + 1) * 32, cols] = xr.astype(BF)
                    half[1, mm, q * 32:(q + 1) * 32, cols] = xi.astype(BF)
        for m in range(4):
            prod = dot(jnp.concatenate([half[0, m], half[1, m]], axis=0), t2[s])
            gbuf[0, :, :] = prod[:, :HALF]
            gbuf[1, :, :] = prod[:, HALF:]
            for i in range(0, QUARTER, 32):
                re, im = slice(i, i + 32), slice(QUARTER + i, QUARTER + i + 32)
                for par in range(2):
                    ln = slice(par * 128, par * 128 + 128)
                    rc, ic = gbuf[0, re, ln], gbuf[0, im, ln]
                    rs_, is_ = gbuf[1, re, ln], gbuf[1, im, ln]
                    pr_, pi_ = rc - is_, ic + rs_
                    mr_, mi_ = rc + is_, ic - rs_
                    if par == 0:
                        first = iota((32, QUARTER), 1) == 0
                        pr_, pi_ = jnp.where(first, rc, pr_), jnp.where(first, ic, pi_)
                        mr_, mi_ = jnp.where(first, rs_, mr_), jnp.where(first, is_, mi_)
                    for k, (a, b) in enumerate([(pr_, pi_), (mr_, mi_)]):
                        tt = 2 * k + par
                        mag = ampp[s, m, i:i + 32, tt * 128:(tt + 1) * 128].astype(F32)
                        factor = mag * lax.rsqrt(jnp.maximum(a * a + b * b, 0.25)) - 1.0
                        dbuf[par, i:i + 32, k * 128:(k + 1) * 128] = (a * factor).astype(BF)
                        dbuf[par, i:i + 32, 256 + k * 128:256 + (k + 1) * 128] = (b * factor).astype(BF)
            e = dot(dbuf[0], t3[s, 0])
            o = dot(dbuf[1], t3[s, 1])
            a, b = e + o, e - o
            back[0, m, :, :HALF] = a[:, :HALF].astype(BF)
            back[1, m, :, :HALF] = a[:, HALF:].astype(BF)
            back[0, m, :, HALF:] = b[:, :HALF].astype(BF)
            back[1, m, :, HALF:] = b[:, HALF:].astype(BF)
        for h in range(2):
            cols = slice(h * HALF, (h + 1) * HALF)
            for m in range(4):
                gbuf[m] = dot(t4[s, m], jnp.concatenate([back[0, m, :, cols], back[1, m, :, cols]], axis=0))
            for i in range(0, QUARTER, 32):
                re, im = slice(i, i + 32), slice(QUARTER + i, QUARTER + i + 32)
                g = [(gbuf[m, re, :], gbuf[m, im, :]) for m in range(4)]
                ar, ai = g[0][0] + g[2][0], g[0][1] + g[2][1]
                br_, bi_ = g[0][0] - g[2][0], g[0][1] - g[2][1]
                cr, ci = g[1][0] + g[3][0], g[1][1] + g[3][1]
                dr, di = g[1][0] - g[3][0], g[1][1] - g[3][1]
                mu = i // 32
                m = (mu - oy) & 3
                for q, (wr, wi) in enumerate([(ar + cr, ai + ci), (br_ - di, bi_ + dr),
                                              (ar - cr, ai - ci), (br_ + di, bi_ - dr)]):
                    rs = slice(q * 32, (q + 1) * 32)
                    pr, pi = prot[s, 0, m, rs, cols], prot[s, 1, m, rs, cols]
                    term[s, 0, mu, rs, cols] = pr * wr + pi * wi
                    term[s, 1, mu, rs, cols] = pr * wi - pi * wr
        return carry

    lax.fori_loop(0, SLOTS, one_slot, 0)

    def down_right(p, m):
        return remote(slr.at[p, m], rlr.at[p, m], bs.at[0, p, m], br.at[0, p, m], down, c)

    def down_left(p, m):
        return remote(sll.at[p, m], rll.at[p, m], bs.at[1, p, m], br.at[1, p, m], down, c)

    def to_right(p, m):
        return remote(sur.at[p, m], rur.at[p, m], bs.at[2, p, m], br.at[2, p, m], r, right)

    for p, m in chunks:
        def gather(i, carry, p=p, m=m):
            rs = pl.ds(pl.multiple_of(i * 16, 16), 16)
            rows = 4 * (iota((16, SIDE), 0) + i * 16) + m
            lanes = iota((16, SIDE), 1)
            al = jnp.zeros((16, SIDE), F32)
            ur, ll, lr = al, al, al
            zero = al
            for s in range(SLOTS):
                x = term[s, p, m, rs, :]
                own_row, own_col = rows >= offy[0, s], lanes >= offx[0, s]
                u = jnp.where(own_row, x, zero)
                l = jnp.where(own_row, zero, x)
                al = al + jnp.where(own_col, u, zero)
                ur = ur + jnp.where(own_col, zero, u)
                ll = ll + jnp.where(own_col, l, zero)
                lr = lr + jnp.where(own_col, zero, l)
            hs[p, m, rs, :] = al
            term[0, p, m, rs, :] = ur
            sll[p, m, rs, :] = ll.astype(BF)
            slr[p, m, rs, :] = lr.astype(BF)
            return carry
        lax.fori_loop(0, QUARTER // 16, gather, 0)
        down_right(p, m).start()
    for p, m in chunks:
        down_left(p, m).start()
    for p, m in chunks:
        down_right(p, m).wait_recv()

        def add_right(i, carry, p=p, m=m):
            rs = pl.ds(pl.multiple_of(i * 16, 16), 16)
            sur[p, m, rs, :] = (term[0, p, m, rs, :] + rlr[p, m, rs, :].astype(F32)).astype(BF)
            return carry
        lax.fori_loop(0, QUARTER // 16, add_right, 0)
        to_right(p, m).start()
    for p, m in chunks:
        down_left(p, m).wait_recv()
        to_right(p, m).wait_recv()
        scale = power[0:1, 0:1]
        for i in range(0, QUARTER, 16):
            rs = slice(i, i + 16)
            sums = hs[p, m, rs, :] + (rll[p, m, rs, :].astype(F32) + rur[p, m, rs, :].astype(F32))
            hs[p, m, rs, :] = strided(objn, p, m + 4 * i, 16) + scale * sums

    lane = iota((QUARTER, QUARTER), 1)
    cols = jnp.zeros((QUARTER, QUARTER), F32)
    for p, m in chunks:
        at = 4 * p + m
        cols = jnp.where(lane == at, pltpu.roll(hs[p, m, :, 0:QUARTER], at, 1), cols)
        cols = jnp.where(lane == 8 + at, pltpu.roll(hs[p, m, :, SIDE - QUARTER:], (8 + at + 1) % QUARTER, 1), cols)
    turned = cols.T
    msg[2] = turned[0:8]
    msg[3] = turned[8:16]
    for p in range(2):
        for k in range(4):
            msg[0, 4 * p + k:4 * p + k + 1, :] = hs[p, 0, 0:1, k * 128:(k + 1) * 128]
            msg[1, 4 * p + k:4 * p + k + 1, :] = hs[p, 3, 127:128, k * 128:(k + 1) * 128]
    plan = [(0, 2, up, left), (0, 1, up, c), (0, 0, up, right),
            (1, 5, down, left), (1, 4, down, c), (1, 3, down, right),
            (2, 6, r, left), (3, 7, r, right)]
    rims = [remote(msg.at[a], halo.at[b], hsem.at[i], hrem.at[i], rr, cc) for i, (a, b, rr, cc) in enumerate(plan)]
    for copy in rims:
        copy.start()
    for copy in rims:
        copy.wait_recv()
    filler = jnp.zeros((QUARTER - 8, QUARTER), F32)
    for k in range(2):
        colt[k, 0:QUARTER, :] = jnp.concatenate([halo[6 + k], filler], axis=0).T

    lane8 = iota((8, QUARTER), 1)
    for k, (src, tl, ln) in enumerate([(2, 0, 0), (0, 3, 127)]):
        row = jnp.zeros((8, QUARTER), F32)
        for p in range(2):
            v = jnp.broadcast_to(halo[src, 4 * p + tl:4 * p + tl + 1, :], (8, QUARTER))
            row = jnp.where(lane8 == 4 * p, pltpu.roll(v, (4 * p - ln) % QUARTER, 1), row)
        colt[k, QUARTER:QUARTER + 8, :] = row

    def out_copy(p, k):
        return pltpu.make_async_copy(outn.at[p, k], (outr, outi)[p].at[:, k * QUARTER:(k + 1) * QUARTER], outsem.at[p, k])

    def partner(x, lanes_odd, shifted, xr=None, xl=None):
        ahead, behind = pltpu.roll(x, SIDE - 1, 1), pltpu.roll(x, 1, 1)
        if not shifted:
            return jnp.where(lanes_odd, behind, ahead)
        q = jnp.where(lanes_odd, ahead, behind)
        ln = iota((x.shape[0], QUARTER), 1)
        return jnp.concatenate([jnp.where(ln == 0, xl, q[:, :128]), q[:, 128:384],
                                jnp.where(ln == 127, xr, q[:, 384:])], axis=1)

    def clipped(x):
        return x - jnp.clip(x, -2 * SHRINK, 2 * SHRINK)

    def clean(a, b, shifted, ar=None, br_=None, al=None, bl=None):
        odd = (iota(a.shape, 1) & 1) == 1
        s, d = a + b, a - b
        if shifted:
            ps = partner(s, odd, True, ar + br_, al + bl)
            pd = partner(d, odd, True, ar - br_, al - bl)
        else:
            ps, pd = partner(s, odd, False), partner(d, odd, False)
        x = (s + ps) + clipped(s - ps)
        y = clipped(d + pd) + clipped(d - pd)
        return x + y, x - y

    for p in range(2):
        ext[0:QUARTER, :] = hs[p, 0]
        for k in range(4):
            ext[QUARTER:QUARTER + 1, k * 128:(k + 1) * 128] = halo[1, 4 * p + k:4 * p + k + 1, :]

        def at_right(rs, m):
            return pltpu.roll(colt[0, rs, :], (127 - (4 * p + m)) % QUARTER, 1)

        def at_left(rs, m):
            return pltpu.roll(colt[1, rs, :], (QUARTER - (4 * p + m)) % QUARTER, 1)

        above = jnp.concatenate([halo[4, 4 * p + k:4 * p + k + 1, :] for k in range(4)], axis=1)
        corner_l = pltpu.roll(jnp.broadcast_to(halo[3, 4 * p + 3:4 * p + 4, :], (8, QUARTER)), 1, 1)
        corner_r = pltpu.roll(jnp.broadcast_to(halo[5, 4 * p:4 * p + 1, :], (8, QUARTER)), 127, 1)
        eight = slice(0, 8)
        _, top = clean(jnp.broadcast_to(above, (8, SIDE)), hs[p, 0, eight, :], True,
                       corner_r, at_right(eight, 0), corner_l, at_left(eight, 0))
        res[0:1, :] = top[0:1, :]
        for i in range(0, QUARTER, 16):
            rs, nx = slice(i, i + 16), slice(i + 1, i + 17)
            x, y = clean(hs[p, 3, rs, :], ext[nx, :], True,
                         at_right(rs, 3), at_right(nx, 0), at_left(rs, 3), at_left(nx, 0))
            res[nx, :] = y
            term[1, 0, 3, rs, :] = x
        for i in range(0, QUARTER, 16):
            rs = slice(i, i + 16)
            x1, x2 = clean(hs[p, 1, rs, :], hs[p, 2, rs, :], True,
                           at_right(rs, 1), at_right(rs, 2), at_left(rs, 1), at_left(rs, 2))
            h0, h1 = clean(hs[p, 0, rs, :], hs[p, 1, rs, :], False)
            h2, h3 = clean(hs[p, 2, rs, :], hs[p, 3, rs, :], False)
            outs = [h0 + res[rs, :], h1 + x1, h2 + x2, h3 + term[1, 0, 3, rs, :]]
            for m in range(4):
                for k in range(4):
                    outn[p, k, pl.ds(m + 4 * i, 16, stride=4), :] = 0.125 * outs[m][:, k * 128:(k + 1) * 128]
        for k in range(4):
            out_copy(p, k).start()
    for p in range(2):
        for k in range(4):
            out_copy(p, k).wait()
    for p, m in chunks:
        for copy in (to_left(p, m), to_up(p, m), pass_up(p, m), down_right(p, m), down_left(p, m), to_right(p, m)):
            copy.wait_send()
    for copy in rims:
        copy.wait_send()


def body(obj_re, obj_im, probe_re, probe_im, amplitude, offset_y, offset_x, counts):
    plane = (SIDE, SIDE)
    classes = (4, QUARTER, SIDE)
    split = (2, 4, SIDE, QUARTER)
    vm = pltpu.VMEM
    scratch = [
        vm(split, F32), vm((4, 2) + classes, BF), vm(split, F32), vm((SLOTS, 2) + classes, F32),
        vm((SLOTS,) + plane, BF), vm((SLOTS,) + classes, BF),
        vm((HALF, SIDE), BF), vm(plane, BF), vm((2 * SIDE, SIDE), BF), vm((SIDE, 2 * SIDE), BF),
        vm((SLOTS, 4, HALF, HALF), BF), vm((SLOTS,) + plane, BF), vm((SLOTS, 2) + plane, BF), vm((SLOTS, 4, HALF, HALF), BF),
        vm((4, HALF, HALF), F32), vm((2,) + classes, BF), vm((2,) + classes, BF), vm((2, QUARTER, SIDE), BF),
        vm((SLOTS, 2) + classes, F32),
    ] + [vm((2,) + classes, BF)] * 6 + [
        vm((2,) + classes, F32), vm((QUARTER + 8, SIDE), F32), vm((QUARTER + 8, SIDE), F32), vm(split, F32),
        vm((4, 8, QUARTER), F32), vm((8, 8, QUARTER), F32), vm((2, QUARTER + 8, QUARTER), F32), vm((8, QUARTER), F32),
        pltpu.SemaphoreType.DMA((21,)), pltpu.SemaphoreType.DMA((2, 4)),
    ] + [pltpu.SemaphoreType.DMA((3, 2, 4))] * 4 + [pltpu.SemaphoreType.DMA((8,))] * 2
    smem = pl.BlockSpec(memory_space=pltpu.SMEM)
    anyw = pl.BlockSpec(memory_space=pl.ANY)
    return pl.pallas_call(
        kernel,
        out_shape=(jax.ShapeDtypeStruct(plane, F32),) * 2,
        in_specs=[smem] * 3 + [anyw] * 9,
        out_specs=(anyw, anyw),
        scratch_shapes=scratch,
        compiler_params=pltpu.CompilerParams(collective_id=0, has_side_effects=True, vmem_limit_bytes=62 << 20),
    )(offset_y, offset_x, counts, obj_re, obj_im, probe_re, probe_im, amplitude, *[jnp.asarray(t) for t in tables()])


def solution(mesh):
    return jax.shard_map(
        body,
        mesh=mesh,
        in_specs=(P("row", "col"), P("row", "col"), P(), P(), P("row", "col", None, None),
                  P("row", "col"), P("row", "col"), P("row", "col")),
        out_specs=(P("row", "col"), P("row", "col")),
        check_vma=False,
    )
```

time: 868 us -> 96 us (0.11)
  local copies, waits for them, and re-layouts: 255 us -> 3.32 us
  starting transfers between devices: 227 us -> 0 us
  matrix products: 165 us -> 0 us
  waiting for transfers between devices: 136 us -> 0 us
  Pallas kernels: 0 us -> 91.2 us
  loops' own time: 40.5 us -> 0 us
  other arithmetic: 34.7 us -> 0 us
    ppermute x8 -> x0, starting transfers between devices: 227 us -> none  [the longest x4 218 us: passed_along(): return lax.ppermute(value, axis, pairs)]
    slice x12 -> x0, local copies, waits for them, and re-layouts: 194 us -> none  [the longest x2 47.7 us: haar_clean(): low_right = field[:, 1::2, 1::2]]
    dot_general x32 -> x0, matrix products: 165 us -> none  [matmul(): return jnp.dot(left_op, right_op, preferred_element_type=jnp.float32)]
    ppermute x8 -> x0, waiting for transfers between devices: 136 us -> none  [the longest x4 132 us: passed_along(): return lax.ppermute(value, axis, pairs)]
    pallas_call x0 -> x1, Pallas kernels: none -> 91.2 us  [body(): pl.pallas_call(kernel, out_shape=(jax.ShapeDtypeStruct(plane, F32),) * 2,...]
    another operation x1 -> x0, loops' own time: 40.5 us -> none  [body(): accumulated = lax.fori_loop(0, live_count, whole_slot, empty_sums)]
    dynamic_update_slice x2 -> x0, local copies, waits for them, and re-layouts: 28.5 us -> none  [whole_slot(): lax.dynamic_update_slice(accumulated, window + update, (anchor, row_at, c...]
    another operation x6 -> x0, local copies, waits for them, and re-layouts: 14.9 us -> none  [the longest x2 11.7 us: haar_clean(): jnp.stack([top_rows, bottom_rows], axis=2)]
  transfers between devices with their start and end apart: 8 -> 0, of which waited for: 5 -> 0; matrix products, arithmetic and copies ran while one was open for 2% -> 0% of each run, Pallas kernels for 0% -> 0%
where the time goes in v1:
time: 96 us; the launch traced here: 95.8 us
  Pallas kernels  91.2 us (95%)
  local copies, waits for them, and re-layouts  3.32 us (3%)
  between operations  1.3 us (1%)
    pallas_call x1, Pallas kernels, body(): pl.pallas_call(kernel, out_shape=(jax.ShapeDtypeStruct(plane, F32),) * 2,...  91.2 us
    unnamed x4, local copies, waits for them, and re-layouts  3.32 us

profile of v1, /device:TPU:0, one launch (start us, length us, event | category | flops | bytes accessed | tf_op | source)
XLA Modules:
  0.0 95.8 jit_solution(11563976027040392063)
XLA Ops:
  1.3 91.2 %shard_map.131 = (f32[512,512]{1,0:T(8,128)}, f32[512,512]{1,0:T(8,128)}) custom-call(s32[1,4]{1,0:T(1,128)} %offy.1, s32[1,4]{1,0:T(1,128)} %offx.1, s32[1,1]{1,0:T(1,128)S(6)} %copy.16.cnt, f32[512,512]{1,0:T(8,128)} %objr.1, f32[512,512]{1,0:T(8,128)} %obji.1, f32[512,512]{1,0:T(8,128)} %prbr.1, f32[512,512]{1,0:T(8,128)} %prbi.1, ...), custom_call_target="tpu_custom_call" | custom-call | tf_op jit(solution)/shard_map/pallas_call | solution.py:450
  92.5 0.0 copy-start
  92.5 2.4 %copy.17 = f32[512,512]{1,0:T(8,128)} copy(f32[512,512]{1,0:T(8,128)} %get-tuple-element.4) | data formatting | bytes 2097152
  94.8 0.0 copy-done
  94.8 1.0 %copy.18 = f32[512,512]{1,0:T(8,128)} copy(f32[512,512]{1,0:T(8,128)S(1)} %copy-done) | data formatting | bytes 2097152
Async XLA Ops:
  92.5 2.4 %copy-start = (f32[512,512]{1,0:T(8,128)S(1)}, f32[512,512]{1,0:T(8,128)}, u32[]{:S(2)}) copy-start(f32[512,512]{1,0:T(8,128)} %get-tuple-element.5) | copy-start | bytes 3145732

commit v2 on v1

v2 whole, which is shorter than its diff:
```python
import math

import jax
import jax.numpy as jnp
import ml_dtypes
import numpy as np
from jax import lax
from jax.experimental import pallas as pl
from jax.experimental.pallas import tpu as pltpu
from jax.sharding import PartitionSpec as P

SIDE = 512
QUARTER = 128
HALF = 256
SLOTS = 4
EPS = 1e-05
STEP = 0.5
SHRINK = 0.2
BF = jnp.bfloat16
F32 = jnp.float32
MESH = pl.DeviceIdType.MESH


def tables():
    phase = np.arange(SIDE) * (2.0 * math.pi / SIDE)
    norming = 1.0 / math.sqrt(SIDE)
    cosine = (np.cos(phase) * norming).astype(np.float32)
    sine = (-np.sin(phase) * norming).astype(np.float32)
    quarter = np.arange(4) * QUARTER
    cosine[quarter[1::2]] = 0.0
    sine[quarter[0::2]] = 0.0

    def entries(rows, cols):
        at = np.outer(rows, cols) % SIDE
        return cosine[at], sine[at]

    natural = np.arange(SIDE)
    by_class = np.concatenate([natural[m::4] for m in range(4)])
    block = np.concatenate([np.arange(m, QUARTER, 4) for m in range(4)])
    even, odd = np.arange(0, HALF, 2), np.arange(1, HALF, 2)
    minus_even = (SIDE - even) % SIDE
    minus_even[0] = HALF
    freq = np.concatenate([even, odd, minus_even, SIDE - odd])
    c, s = entries(block, by_class)
    first = np.concatenate([c, s], axis=0)
    c, s = entries(natural, freq[:HALF])
    s[:, 0] = entries(natural, np.array([HALF]))[0][:, 0]
    second = np.concatenate([c, s], axis=1)
    c, s = entries(freq, natural)
    third = np.concatenate([c, s], axis=0)
    c, s = entries(natural, by_class)
    fourth = np.concatenate([c, s], axis=1)
    return [t.astype(ml_dtypes.bfloat16) for t in (first, second, third, fourth)]


def dot(a, b):
    return jnp.dot(a, b, preferred_element_type=F32)


def iota(shape, dim):
    return lax.broadcasted_iota(jnp.int32, shape, dim)


def strided(ref, p, start, size):
    return jnp.concatenate([ref[p, k, pl.ds(start, size, stride=4), :] for k in range(4)], axis=1)


def one_hot(hit):
    return jnp.where(hit, 1.0, 0.0).astype(BF)


ORDER = (0, 3, 1, 2)
BLOCKS = (0, 3, 2, 1)


def butterfly(g, sign):
    ar, ai = g[0][0] + g[2][0], g[0][1] + g[2][1]
    br, bi = g[0][0] - g[2][0], g[0][1] - g[2][1]
    cr, ci = g[1][0] + g[3][0], g[1][1] + g[3][1]
    dr, di = g[1][0] - g[3][0], g[1][1] - g[3][1]
    one = (br - di, bi + dr)
    three = (br + di, bi - dr)
    if sign < 0:
        one, three = three, one
    return [(ar + cr, ai + ci), one, (ar - cr, ai - ci), three]


def kernel(offy, offx, cnt, objr, obji, prbr, prbi, amp, b1h, b2h, b3h, b4h,
           hs, rim,
           objn, tile0, tile1, tile2, tile3, prbn, prot, ampr, ampp, b1, b2, b3, b4,
           t1, t2, t3, t4, gbuf, gtwo, hb, dbuf, term,
           slr, sur, sll, rlr, rll, rur, urf,
           msg, halo, side, beside, power,
           insem, fs, fr, bs, br, hsem, hrem):
    tile = (tile0, tile1, tile2, tile3)
    nr, nc = lax.axis_size("row"), lax.axis_size("col")
    r, c = lax.axis_index("row"), lax.axis_index("col")
    up, down = lax.rem(r + nr - 1, nr), lax.rem(r + 1, nr)
    left, right = lax.rem(c + nc - 1, nc), lax.rem(c + 1, nc)

    moves = []
    for pair, dst in (((objr, obji), objn), ((prbr, prbi), prbn)):
        moves += [(pair[p].at[:, k * QUARTER:(k + 1) * QUARTER], dst.at[p, k]) for k in range(4) for p in range(2)]
    moves += [(b1h, b1), (amp.at[0], ampr), (b2h, b2), (b3h, b3), (b4h, b4)]
    ins = [pltpu.make_async_copy(a, b, insem.at[i]) for i, (a, b) in enumerate(moves)]
    for copy in ins:
        copy.start()

    barrier = pltpu.get_barrier_semaphore()
    for rr, cc in ((up, c), (down, c), (r, left), (r, right)):
        pl.semaphore_signal(barrier, inc=1, device_id=(rr, cc), device_id_type=MESH)

    def remote(src, dst, ssem, rsem, rr, cc):
        return pltpu.make_async_remote_copy(src_ref=src, dst_ref=dst, send_sem=ssem, recv_sem=rsem,
                                            device_id=(rr, cc), device_id_type=MESH)

    def to_left(k, p):
        return remote(tile[k].at[0, p], tile[k].at[1, p], fs.at[0, k, p], fr.at[0, k, p], r, left)

    def to_up(k, p):
        return remote(tile[k].at[0, p], tile[k].at[2, p], fs.at[1, k, p], fr.at[1, k, p], up, c)

    def pass_up(k, p):
        return remote(tile[k].at[1, p], tile[k].at[3, p], fs.at[2, k, p], fr.at[2, k, p], up, c)

    for k in range(4):
        for p in range(2):
            ins[2 * k + p].wait()
            for m in range(4):
                tile[k][0, p, m] = objn[p, k, pl.ds(m, QUARTER, stride=4), :].astype(BF)
            if k == 0 and p == 0:
                pl.semaphore_wait(barrier, 4)
            to_left(k, p).start()
            to_up(k, p).start()
    for copy in ins[8:]:
        copy.wait()

    total = jnp.zeros((8, SIDE), F32)
    for p in range(2):
        def add(i, acc, p=p):
            x = jnp.concatenate([prbn[p, k, pl.ds(pl.multiple_of(i * 8, 8), 8), :] for k in range(4)], axis=1)
            return acc + x * x
        total = lax.fori_loop(0, SIDE // 8, add, total)
    mean = jnp.sum(jnp.sum(total, axis=1, keepdims=True), axis=0, keepdims=True) * (1.0 / (SIDE * SIDE)) + EPS
    power[...] = jnp.broadcast_to(STEP / mean, (8, QUARTER))

    def prepare(s):
        oy, ox = offy[0, s], offx[0, s]
        live = jnp.where(s < cnt[0, 0], 1.0, 0.0).astype(F32)
        lam, freq = iota((SIDE, SIDE), 1), iota((SIDE, SIDE), 0)
        lane = lam & 127
        even_minus = jnp.where(lane == 0, HALF, SIDE - 2 * lane)
        want = jnp.where(lam < 128, 2 * lane,
                         jnp.where(lam < 256, 2 * lane + 1,
                                   jnp.where(lam < 384, even_minus, SIDE - 1 - 2 * lane)))
        mixed = dot(ampr[s], one_hot(freq == want)).astype(BF)
        pick = one_hot(lam == 4 * (freq & 127) + (freq >> 7))
        ampp[s] = dot(pick, mixed).astype(BF).reshape(4, QUARTER, SIDE)
        for m in range(4):
            turn = lax.shift_right_logical(oy + m, 2) & 127
            for p in range(2):
                x = strided(prbn, p, m, QUARTER) * live
                x = pltpu.roll(pltpu.roll(x, turn, 0), ox, 1)
                for k in range(4):
                    prot[s, k, p, m] = x[:, k * QUARTER:(k + 1) * QUARTER]
            cs = pltpu.roll(b1[:, m * QUARTER:(m + 1) * QUARTER].astype(F32), turn, 1)
            cc, ss = cs[:QUARTER], cs[QUARTER:]
            t1[s, m] = jnp.concatenate([jnp.concatenate([cc, -ss], axis=1),
                                        jnp.concatenate([ss, cc], axis=1)], axis=0).astype(BF)
        rows, cols = iota((SIDE, SIDE), 0), iota((SIDE, SIDE), 1)
        t2[s] = dot(one_hot(cols == ((rows - ox) & 511)), b2[...]).astype(BF)
        rows, cols = iota((SIDE, HALF), 0), iota((SIDE, HALF), 1)
        cs = dot(b3[...], one_hot(rows == ((cols - ox) & 511)))
        for par in range(2):
            a = par * QUARTER
            cc = jnp.concatenate([cs[a:a + 128], cs[a + 256:a + 384]], axis=0)
            ss = jnp.concatenate([cs[a + 512:a + 640], cs[a + 768:a + 896]], axis=0)
            t3[s, par] = jnp.concatenate([jnp.concatenate([cc, -ss], axis=1),
                                          jnp.concatenate([ss, cc], axis=1)], axis=0).astype(BF)
        rows, cols = iota((QUARTER, SIDE), 0), iota((QUARTER, SIDE), 1)
        place = 4 * (rows & 31) + lax.shift_right_logical(rows, 5)
        cs = dot(one_hot(cols == ((place - oy) & 511)), b4[...])
        for m in range(4):
            cc = cs[:, m * QUARTER:(m + 1) * QUARTER]
            ss = cs[:, SIDE + m * QUARTER:SIDE + (m + 1) * QUARTER]
            t4[s, m] = jnp.concatenate([jnp.concatenate([cc, ss], axis=1),
                                        jnp.concatenate([-ss, cc], axis=1)], axis=0).astype(BF)

    def hand_on(k):
        for p in range(2):
            to_left(k, p).wait_recv()
            pass_up(k, p).start()

    def arrived(k):
        for p in range(2):
            to_up(k, p).wait_recv()
        for p in range(2):
            pass_up(k, p).wait_recv()

    def first_stage(k0, nk):
        wide = nk * QUARTER
        cols = slice(k0 * QUARTER, k0 * QUARTER + wide)

        def wider(read):
            return jnp.concatenate([read(k) for k in range(k0, k0 + nk)], axis=1)

        def one(s, carry):
            oy, ox = offy[0, s], offx[0, s]
            for m in range(4):
                mu = (m + oy) & 3
                xs = []
                for i in range(0, QUARTER, 32):
                    rs = slice(i, i + 32)
                    own_row = 4 * (iota((32, wide), 0) + i) + mu >= oy
                    own_col = iota((32, wide), 1) + k0 * QUARTER >= ox
                    part = []
                    for p in range(2):
                        q = [wider(lambda k, j=j: tile[k][j, p, mu, rs, :]).astype(F32) for j in range(4)]
                        part.append(jnp.where(own_row, jnp.where(own_col, q[0], q[1]),
                                              jnp.where(own_col, q[2], q[3])))
                    pr, pi = [wider(lambda k, p=p: prot[s, k, p, m, rs, :]) for p in range(2)]
                    xs.append(((pr * part[0] - pi * part[1]).astype(BF), (pr * part[1] + pi * part[0]).astype(BF)))
                x = jnp.concatenate([a for a, _ in xs] + [b for _, b in xs], axis=0)
                gbuf[m, :, :wide] = dot(t1[s, m], x)
            for i in range(0, QUARTER, 32):
                re, im = slice(i, i + 32), slice(QUARTER + i, QUARTER + i + 32)
                outs = butterfly([(gbuf[m, re, :wide], gbuf[m, im, :wide]) for m in range(4)], -1)
                for q, (xr, xi) in enumerate(outs):
                    hb[s, 0, i // 32, q * 32:(q + 1) * 32, cols] = xr.astype(BF)
                    hb[s, 1, i // 32, q * 32:(q + 1) * 32, cols] = xi.astype(BF)
            return carry

        lax.fori_loop(0, SLOTS, one, 0)

    def prepare_and_pass(s, carry):
        prepare(s)
        for k in range(2):
            @pl.when(s == k)
            def _(k=k):
                hand_on(k)
        return carry

    lax.fori_loop(0, SLOTS, prepare_and_pass, 0)
    hand_on(2)
    arrived(0)
    arrived(1)
    first_stage(0, 2)
    hand_on(3)
    arrived(2)
    first_stage(2, 1)
    arrived(3)
    first_stage(3, 1)

    def middle(s, carry):
        def spectrum(m):
            prod = dot(jnp.concatenate([hb[s, 0, m], hb[s, 1, m]], axis=0), t2[s])
            gtwo[m % 2, 0] = prod[:, :HALF]
            gtwo[m % 2, 1] = prod[:, HALF:]

        spectrum(0)
        for m in range(4):
            if m < 3:
                spectrum(m + 1)
            g, d = gtwo.at[m % 2], dbuf.at[m % 2]
            for i in range(0, QUARTER, 32):
                re, im = slice(i, i + 32), slice(QUARTER + i, QUARTER + i + 32)
                for par in range(2):
                    ln = slice(par * 128, par * 128 + 128)
                    rc, ic = g[0, re, ln], g[0, im, ln]
                    rs_, is_ = g[1, re, ln], g[1, im, ln]
                    pr_, pi_ = rc - is_, ic + rs_
                    mr_, mi_ = rc + is_, ic - rs_
                    if par == 0:
                        first = iota((32, QUARTER), 1) == 0
                        pr_, pi_ = jnp.where(first, rc, pr_), jnp.where(first, ic, pi_)
                        mr_, mi_ = jnp.where(first, rs_, mr_), jnp.where(first, is_, mi_)
                    for k, (a, b) in enumerate([(pr_, pi_), (mr_, mi_)]):
                        tt = 2 * k + par
                        mag = ampp[s, m, i:i + 32, tt * 128:(tt + 1) * 128].astype(F32)
                        factor = mag * lax.rsqrt(jnp.maximum(a * a + b * b, 0.25)) - 1.0
                        d[par, i:i + 32, k * 128:(k + 1) * 128] = (a * factor).astype(BF)
                        d[par, i:i + 32, 256 + k * 128:256 + (k + 1) * 128] = (b * factor).astype(BF)
            e = dot(d[0], t3[s, 0])
            o = dot(d[1], t3[s, 1])
            a, b = e + o, e - o
            hb[s, 0, m, :, :HALF] = a[:, :HALF].astype(BF)
            hb[s, 1, m, :, :HALF] = a[:, HALF:].astype(BF)
            hb[s, 0, m, :, HALF:] = b[:, :HALF].astype(BF)
            hb[s, 1, m, :, HALF:] = b[:, HALF:].astype(BF)
        return carry

    lax.fori_loop(0, SLOTS, middle, 0)

    def down_right(k, j):
        return remote(slr.at[k, j], rlr.at[k, j], bs.at[0, k, j], br.at[0, k, j], down, c)

    def down_left(k, j):
        return remote(sll.at[k, j], rll.at[k, j], bs.at[1, k, j], br.at[1, k, j], down, c)

    def to_right(k, j):
        return remote(sur.at[k, j], rur.at[k, j], bs.at[2, k, j], br.at[2, k, j], r, right)

    def lanes_of(k):
        return pl.ds(pl.multiple_of(k * QUARTER, QUARTER), QUARTER)

    def last_stage(kk, carry):
        k = lax.rem(3 * kk, 4)
        cols = lanes_of(k)

        def one(s, inner):
            oy = offy[0, s]
            for m in range(4):
                x = jnp.concatenate([hb[s, 0, m, :, cols], hb[s, 1, m, :, cols]], axis=0)
                gbuf[m, :, :QUARTER] = dot(t4[s, m], x)
            for i in range(0, QUARTER, 32):
                re, im = slice(i, i + 32), slice(QUARTER + i, QUARTER + i + 32)
                outs = butterfly([(gbuf[m, re, :QUARTER], gbuf[m, im, :QUARTER]) for m in range(4)], 1)
                mu = i // 32
                m = (mu - oy) & 3
                for q, (wr, wi) in enumerate(outs):
                    rs = slice(q * 32, (q + 1) * 32)
                    pr, pi = prot[s, k, 0, m, rs, :], prot[s, k, 1, m, rs, :]
                    term[s, 0, mu, rs, :] = pr * wr + pi * wi
                    term[s, 1, mu, rs, :] = pr * wi - pi * wr
            return inner

        lax.fori_loop(0, SLOTS, one, 0)
        zero = jnp.zeros((32, QUARTER), F32)
        lanes = iota((32, QUARTER), 1) + k * QUARTER
        for at, m in enumerate(ORDER):
            j, n = at // 2, at % 2
            for i in range(0, QUARTER, 32):
                rs = slice(i, i + 32)
                rows = 4 * (iota((32, QUARTER), 0) + i) + m
                for p in range(2):
                    al, ur, ll, lr = zero, zero, zero, zero
                    for s in range(SLOTS):
                        x = term[s, p, m, rs, :]
                        own_row, own_col = rows >= offy[0, s], lanes >= offx[0, s]
                        u = jnp.where(own_row, x, zero)
                        l = jnp.where(own_row, zero, x)
                        al = al + jnp.where(own_col, u, zero)
                        ur = ur + jnp.where(own_col, zero, u)
                        ll = ll + jnp.where(own_col, l, zero)
                        lr = lr + jnp.where(own_col, zero, l)
                    hs[p, m, rs, cols] = al
                    urf[k, j, n, p, rs, :] = ur
                    sll[k, j, n, p, rs, :] = ll.astype(BF)
                    slr[k, j, n, p, rs, :] = lr.astype(BF)
            if at == 1:
                down_right(k, 0).start()

        @pl.when(kk > 0)
        def _():
            add_right(lax.rem(3 * kk + 1, 4), 0)
        return carry

    def add_right(k, j):
        down_right(k, j).wait_recv()
        for n in range(2):
            for p in range(2):
                sur[k, j, n, p] = (urf[k, j, n, p] + rlr[k, j, n, p].astype(F32)).astype(BF)
        to_right(k, j).start()

    lax.fori_loop(0, 4, last_stage, 0)
    for k in BLOCKS:
        down_right(k, 1).start()
    add_right(1, 0)
    for k in BLOCKS:
        down_left(k, 0).start()
    add_right(0, 1)
    add_right(3, 1)
    for k in BLOCKS:
        down_left(k, 1).start()
    add_right(2, 1)
    add_right(1, 1)

    def row_rims(k):
        return [remote(msg.at[2 * k + d], halo.at[2 * k + d], hsem.at[2 * k + d], hrem.at[2 * k + d], rr, c)
                for d, rr in ((0, up), (1, down))]

    def column_rim(k):
        n, cc = (0, left) if k == 0 else (1, right)
        return remote(side.at[n], beside.at[n], hsem.at[8 + n], hrem.at[8 + n], r, cc)

    scale = power[0:1, 0:1]
    for j in range(2):
        for k in BLOCKS:
            cols = slice(k * QUARTER, (k + 1) * QUARTER)
            down_left(k, j).wait_recv()
            to_right(k, j).wait_recv()
            for n in range(2):
                m = ORDER[2 * j + n]
                for p in range(2):
                    for i in range(0, QUARTER, 64):
                        rs = slice(i, i + 64)
                        sums = hs[p, m, rs, cols] + (rll[k, j, n, p, rs, :].astype(F32) + rur[k, j, n, p, rs, :].astype(F32))
                        hs[p, m, rs, cols] = objn[p, k, pl.ds(m + 4 * i, 64, stride=4), :] + scale * sums
            if j == 0:
                for p in range(2):
                    msg[2 * k, p:p + 1, :] = hs[p, 0, 0:1, cols]
                    msg[2 * k + 1, p:p + 1, :] = hs[p, 3, 127:128, cols]
                for copy in row_rims(k):
                    copy.start()
            elif k in (0, 3):
                lane = iota((QUARTER, QUARTER), 1)
                edge = jnp.zeros((QUARTER, QUARTER), F32)
                for at in range(8):
                    turn = at if k == 0 else (at + 1) % QUARTER
                    edge = jnp.where(lane == at, pltpu.roll(hs[at // 4, at % 4, :, cols], turn, 1), edge)
                side[k // 3, 0:8, :] = edge.T[0:8]
                for copy in row_rims(k):
                    copy.wait_recv()
                side[k // 3, 8:16, :] = halo[2 * k]
                side[k // 3, 16:24, :] = halo[2 * k + 1]
                column_rim(k).start()
    for k in (1, 2):
        for copy in row_rims(k):
            copy.wait_recv()
    for k in (0, 3):
        column_rim(k).wait_recv()
    rim[0:8] = halo[...]
    for n in range(2):
        for g in range(3):
            rim[8 + 3 * n + g] = beside[n, 8 * g:8 * g + 8, :]

    for k in range(4):
        for p in range(2):
            for copy in (to_left(k, p), to_up(k, p), pass_up(k, p), down_right(k, p), down_left(k, p), to_right(k, p)):
                copy.wait_send()
        for copy in row_rims(k):
            copy.wait_send()
    for k in (0, 3):
        column_rim(k).wait_send()


def clean_kernel(hs, halo, outr, outi, ext, res, last, outn, colt, outsem):
    filler = jnp.zeros((QUARTER - 8, QUARTER), F32)
    for k in range(2):
        colt[k, 0:QUARTER, :] = jnp.concatenate([halo[8 + 3 * k], filler], axis=0).T

    lane8 = iota((8, QUARTER), 1)
    for k, (src, ln) in enumerate([(9, 0), (12, 127)]):
        row = jnp.zeros((8, QUARTER), F32)
        for p in range(2):
            v = jnp.broadcast_to(halo[src, p:p + 1, :], (8, QUARTER))
            row = jnp.where(lane8 == 4 * p, pltpu.roll(v, (4 * p - ln) % QUARTER, 1), row)
        colt[k, QUARTER:QUARTER + 8, :] = row

    def out_copy(p, k):
        return pltpu.make_async_copy(outn.at[p, k], (outr, outi)[p].at[:, k * QUARTER:(k + 1) * QUARTER], outsem.at[p, k])

    def out_part(p, k, i):
        rs = pl.ds(4 * i - 64, 128)
        return pltpu.make_async_copy(outn.at[p, k, rs], (outr, outi)[p].at[rs, k * QUARTER:(k + 1) * QUARTER], outsem.at[p, k])

    def partner(x, lanes_odd, shifted, xr=None, xl=None):
        ahead, behind = pltpu.roll(x, SIDE - 1, 1), pltpu.roll(x, 1, 1)
        if not shifted:
            return jnp.where(lanes_odd, behind, ahead)
        q = jnp.where(lanes_odd, ahead, behind)
        ln = iota((x.shape[0], QUARTER), 1)
        return jnp.concatenate([jnp.where(ln == 0, xl, q[:, :128]), q[:, 128:384],
                                jnp.where(ln == 127, xr, q[:, 384:])], axis=1)

    def clipped(x):
        return x - jnp.clip(x, -2 * SHRINK, 2 * SHRINK)

    def clean(a, b, shifted, ar=None, br_=None, al=None, bl=None):
        odd = (iota(a.shape, 1) & 1) == 1
        s, d = a + b, a - b
        if shifted:
            ps = partner(s, odd, True, ar + br_, al + bl)
            pd = partner(d, odd, True, ar - br_, al - bl)
        else:
            ps, pd = partner(s, odd, False), partner(d, odd, False)
        x = (s + ps) + clipped(s - ps)
        y = clipped(d + pd) + clipped(d - pd)
        return x + y, x - y

    for p in range(2):
        ext[0:QUARTER, :] = hs[p, 0]
        for k in range(4):
            ext[QUARTER:QUARTER + 1, k * 128:(k + 1) * 128] = halo[2 * k, p:p + 1, :]

        def at_right(rs, m):
            return pltpu.roll(colt[0, rs, :], (127 - (4 * p + m)) % QUARTER, 1)

        def at_left(rs, m):
            return pltpu.roll(colt[1, rs, :], (QUARTER - (4 * p + m)) % QUARTER, 1)

        above = jnp.concatenate([halo[2 * k + 1, p:p + 1, :] for k in range(4)], axis=1)
        corner_l = pltpu.roll(jnp.broadcast_to(halo[13, p:p + 1, :], (8, QUARTER)), 1, 1)
        corner_r = pltpu.roll(jnp.broadcast_to(halo[10, p:p + 1, :], (8, QUARTER)), 127, 1)
        eight = slice(0, 8)
        _, top = clean(jnp.broadcast_to(above, (8, SIDE)), hs[p, 0, eight, :], True,
                       corner_r, at_right(eight, 0), corner_l, at_left(eight, 0))
        res[0:1, :] = top[0:1, :]
        for i in range(0, QUARTER, 16):
            rs, nx = slice(i, i + 16), slice(i + 1, i + 17)
            x, y = clean(hs[p, 3, rs, :], ext[nx, :], True,
                         at_right(rs, 3), at_right(nx, 0), at_left(rs, 3), at_left(nx, 0))
            res[nx, :] = y
            last[rs, :] = x
        for i in range(0, QUARTER, 16):
            rs = slice(i, i + 16)
            x1, x2 = clean(hs[p, 1, rs, :], hs[p, 2, rs, :], True,
                           at_right(rs, 1), at_right(rs, 2), at_left(rs, 1), at_left(rs, 2))
            h0, h1 = clean(hs[p, 0, rs, :], hs[p, 1, rs, :], False)
            h2, h3 = clean(hs[p, 2, rs, :], hs[p, 3, rs, :], False)
            outs = [h0 + res[rs, :], h1 + x1, h2 + x2, h3 + last[rs, :]]
            for m in range(4):
                for k in range(4):
                    outn[p, k, pl.ds(m + 4 * i, 16, stride=4), :] = 0.125 * outs[m][:, k * 128:(k + 1) * 128]
            if i % 32 == 16:
                for k in range(4):
                    out_part(p, k, i).start()
    for p in range(2):
        for k in range(4):
            out_copy(p, k).wait()


def body(obj_re, obj_im, probe_re, probe_im, amplitude, offset_y, offset_x, counts):
    plane = (SIDE, SIDE)
    classes = (4, QUARTER, SIDE)
    square = (QUARTER, QUARTER)
    split = (2, 4, SIDE, QUARTER)
    vm = pltpu.VMEM
    scratch = [
        vm(split, F32), *[vm((4, 2, 4) + square, BF)] * 4, vm(split, F32), vm((SLOTS, 4, 2, 4) + square, F32),
        vm((SLOTS,) + plane, BF), vm((SLOTS,) + classes, BF),
        vm((HALF, SIDE), BF), vm(plane, BF), vm((2 * SIDE, SIDE), BF), vm((SIDE, 2 * SIDE), BF),
        vm((SLOTS, 4, HALF, HALF), BF), vm((SLOTS,) + plane, BF), vm((SLOTS, 2) + plane, BF), vm((SLOTS, 4, HALF, HALF), BF),
        vm((4, HALF, HALF), F32), vm((2, 2, HALF, HALF), F32), vm((SLOTS, 2) + classes, BF), vm((2, 2, QUARTER, SIDE), BF),
        vm((SLOTS, 2, 4) + square, F32),
    ] + [vm((4, 2, 2, 2) + square, BF)] * 6 + [
        vm((4, 2, 2, 2) + square, F32),
        vm((8, 8, QUARTER), F32), vm((8, 8, QUARTER), F32), vm((2, 24, QUARTER), F32), vm((2, 24, QUARTER), F32), vm((8, QUARTER), F32),
        pltpu.SemaphoreType.DMA((21,)),
    ] + [pltpu.SemaphoreType.DMA((3, 4, 2))] * 4 + [pltpu.SemaphoreType.DMA((10,))] * 2
    smem = pl.BlockSpec(memory_space=pltpu.SMEM)
    anyw = pl.BlockSpec(memory_space=pl.ANY)
    onchip = pl.BlockSpec(memory_space=pltpu.VMEM)
    hs, rim = pl.pallas_call(
        kernel,
        out_shape=(pltpu.VMEM((2,) + classes, F32), pltpu.VMEM((14, 8, QUARTER), F32)),
        in_specs=[smem] * 3 + [anyw] * 9,
        out_specs=(onchip, onchip),
        scratch_shapes=scratch,
        compiler_params=pltpu.CompilerParams(collective_id=0, has_side_effects=True, vmem_limit_bytes=60 << 20),
    )(offset_y, offset_x, counts, obj_re, obj_im, probe_re, probe_im, amplitude, *[jnp.asarray(t) for t in tables()])
    return pl.pallas_call(
        clean_kernel,
        out_shape=(jax.ShapeDtypeStruct(plane, F32),) * 2,
        in_specs=[onchip, onchip],
        out_specs=(anyw, anyw),
        scratch_shapes=[vm((QUARTER + 8, SIDE), F32), vm((QUARTER + 8, SIDE), F32), vm((QUARTER, SIDE), F32),
                        vm(split, F32), vm((2, QUARTER + 8, QUARTER), F32), pltpu.SemaphoreType.DMA((2, 4))],
        compiler_params=pltpu.CompilerParams(vmem_limit_bytes=16 << 20),
    )(hs, rim)


def solution(mesh):
    return jax.shard_map(
        body,
        mesh=mesh,
        in_specs=(P("row", "col"), P("row", "col"), P(), P(), P("row", "col", None, None),
                  P("row", "col"), P("row", "col"), P("row", "col")),
        out_specs=(P("row", "col"), P("row", "col")),
        check_vma=False,
    )
```

time: 96 us -> 83.9 us (0.87)
  Pallas kernels: 91.2 us -> 82.5 us
  local copies, waits for them, and re-layouts: 3.32 us -> 0 us
    pallas_call x1 -> x2, Pallas kernels: 91.2 us -> 82.5 us  [the longest x1 79.1 us: body(): pl.pallas_call(kernel, out_shape=(pltpu.VMEM((2,) + classes, F32), pltpu....]
    unnamed x4 -> x0, local copies, waits for them, and re-layouts: 3.32 us -> none
where the time goes in v2:
time: 83.9 us; the launch traced here: 83.8 us
  Pallas kernels  82.5 us (98%)
  between operations  1.29 us (2%)
    pallas_call x1, Pallas kernels, body(): pl.pallas_call(kernel, out_shape=(pltpu.VMEM((2,) + classes, F32), pltpu....  79.1 us
    pallas_call x1, Pallas kernels, body(): pl.pallas_call(clean_kernel, out_shape=(jax.ShapeDtypeStruct(plane, F32),...  3.4 us

profile of v2, /device:TPU:0, one launch (start us, length us, event | category | flops | bytes accessed | tf_op | source)
XLA Modules:
  0.0 83.8 jit_solution(13707723349400238984)
XLA Ops:
  1.3 79.1 %shard_map.131 = (f32[2,4,128,512]{3,2,1,0:T(8,128)S(1)}, f32[14,8,128]{2,1,0:T(8,128)S(1)}) custom-call(s32[1,4]{1,0:T(1,128)} %offy.1, s32[1,4]{1,0:T(1,128)} %offx.1, s32[1,1]{1,0:T(1,128)S(6)} %copy.14.cnt, f32[512,512]{1,0:T(8,128)} %objr.1, f32[512,512]{1,0:T(8,128)} %obji.1, f32[512,512]{1,0:T(8,128)} %prbr.1, f32[512,512]{1,0:T(8,128)} %prbi.1, ...), custom_call_target="tpu_custom_call" | custom-call | tf_op jit(solution)/shard_map/pallas_call | solution.py:544
  80.4 3.4 %shard_map.132 = (f32[512,512]{1,0:T(8,128)}, f32[512,512]{1,0:T(8,128)}) custom-call(f32[2,4,128,512]{3,2,1,0:T(8,128)S(1)} %get-tuple-element.4.hs, f32[14,8,128]{2,1,0:T(8,128)S(1)} %get-tuple-element.5.halo), custom_call_target="tpu_custom_call" | custom-call | tf_op jit(solution)/shard_map/pallas_call | solution.py:552

commit v3 on v2

--- a/solution.py
+++ b/solution.py
@@ -215,9 +215,9 @@
                     own_col = iota((32, wide), 1) + k0 * QUARTER >= ox
                     part = []
                     for p in range(2):
-                        q = [wider(lambda k, j=j: tile[k][j, p, mu, rs, :]).astype(F32) for j in range(4)]
+                        q = [wider(lambda k, j=j: tile[k][j, p, mu, rs, :]) for j in range(4)]
                         part.append(jnp.where(own_row, jnp.where(own_col, q[0], q[1]),
-                                              jnp.where(own_col, q[2], q[3])))
+                                              jnp.where(own_col, q[2], q[3])).astype(F32))
                     pr, pi = [wider(lambda k, p=p: prot[s, k, p, m, rs, :]) for p in range(2)]
                     xs.append(((pr * part[0] - pi * part[1]).astype(BF), (pr * part[1] + pi * part[0]).astype(BF)))
                 x = jnp.concatenate([a for a, _ in xs] + [b for _, b in xs], axis=0)
@@ -374,6 +374,10 @@
         down_left(k, 1).start()
     add_right(2, 1)
     add_right(1, 1)
+    for k in range(4):
+        for p in range(2):
+            for copy in (to_left(k, p), to_up(k, p), pass_up(k, p), down_right(k, p)):
+                copy.wait_send()
 
     def row_rims(k):
         return [remote(msg.at[2 * k + d], halo.at[2 * k + d], hsem.at[2 * k + d], hrem.at[2 * k + d], rr, c)
@@ -420,14 +424,12 @@
     for k in (0, 3):
         column_rim(k).wait_recv()
     rim[0:8] = halo[...]
-    for n in range(2):
-        for g in range(3):
-            rim[8 + 3 * n + g] = beside[n, 8 * g:8 * g + 8, :]
+    rim[8:14] = beside[...].reshape(6, 8, QUARTER)
 
     for k in range(4):
         for p in range(2):
-            for copy in (to_left(k, p), to_up(k, p), pass_up(k, p), down_right(k, p), down_left(k, p), to_right(k, p)):
-                copy.wait_send()
+            down_left(k, p).wait_send()
+            to_right(k, p).wait_send()
         for copy in row_rims(k):
             copy.wait_send()
     for k in (0, 3):

time: 83.9 us -> 83.6 us (level)
  no operation moved by 1% of the time
where the time goes in v3:
time: 83.6 us; the launch traced here: 83.4 us
  Pallas kernels  82.1 us (98%)
  between operations  1.29 us (2%)
    pallas_call x1, Pallas kernels, body(): pl.pallas_call(kernel, out_shape=(pltpu.VMEM((2,) + classes, F32), pltpu....  78.7 us
    pallas_call x1, Pallas kernels, body(): pl.pallas_call(clean_kernel, out_shape=(jax.ShapeDtypeStruct(plane, F32),...  3.4 us

profile of v3, /device:TPU:0, one launch (start us, length us, event | category | flops | bytes accessed | tf_op | source)
XLA Modules:
  0.0 83.4 jit_solution(7071937487490661928)
XLA Ops:
  1.3 78.7 %shard_map.131 = (f32[2,4,128,512]{3,2,1,0:T(8,128)S(1)}, f32[14,8,128]{2,1,0:T(8,128)S(1)}) custom-call(s32[1,4]{1,0:T(1,128)} %offy.1, s32[1,4]{1,0:T(1,128)} %offx.1, s32[1,1]{1,0:T(1,128)S(6)} %copy.14.cnt, f32[512,512]{1,0:T(8,128)} %objr.1, f32[512,512]{1,0:T(8,128)} %obji.1, f32[512,512]{1,0:T(8,128)} %prbr.1, f32[512,512]{1,0:T(8,128)} %prbi.1, ...), custom_call_target="tpu_custom_call" | custom-call | tf_op jit(solution)/shard_map/pallas_call | solution.py:546
  80.0 3.4 %shard_map.132 = (f32[512,512]{1,0:T(8,128)}, f32[512,512]{1,0:T(8,128)}) custom-call(f32[2,4,128,512]{3,2,1,0:T(8,128)S(1)} %get-tuple-element.4.hs, f32[14,8,128]{2,1,0:T(8,128)S(1)} %get-tuple-element.5.halo), custom_call_target="tpu_custom_call" | custom-call | tf_op jit(solution)/shard_map/pallas_call | solution.py:554
